TPU v7x, 128 devices: a whole 4x4x4 slice. The times are simulated.
128 devices in a mesh: mp: 2 (over x_hi), gx: 8 (over z, x_lo), gy: 8 (over y, core).
Axes of the slice: x: 4 (x_hi: 2, x_lo: 2; x = x_hi * 2 + x_lo), y: 4, z: 4, core: 2. Of those that a mesh axis runs over, the one named last changes fastest.
Arguments:
- spectrum: float32 [1152, 16384], P(None, ('mp', 'gx', 'gy')), may hold values from 0.25 to 4
- source_weights: bfloat16 [4, 1152, 1152], replicated, may hold values from -0.1875 to 0.1875
- drift_weights: bfloat16 [64, 1152], replicated, may hold values from -0.1875 to 0.1875
- courant: float32 [2, 1152], replicated, may hold values from -0.45 to 0.45
- point_tile: int32 [16384, 1], P(('mp', 'gx', 'gy')), may hold values from 0 to 127; in each aligned block of 128 rows (0 to 127, 128 to 255, ...) at most 2 rows name the same one
- point_cell: int32 [16384], P(('mp', 'gx', 'gy')), may hold values from 0 to 16383
- wave_land: int32 [16384], P(('mp', 'gx', 'gy')), may hold values 0 or 1
- ocean_vel: float32 [2, 32, 2048, 1024], P(None, None, ('mp', 'gx'), 'gy'), may hold values from -6 to 6
- ocean_land: int32 [2048, 1024], P(('mp', 'gx'), 'gy'), may hold values 0 or 1
Outputs:
- energy: float32 [1152, 16384], P(None, ('mp', 'gx', 'gy'))
- ocean_out: float32 [2, 32, 2048, 1024], P(None, None, ('mp', 'gx'), 'gy')
Inputs may be any that keep to these rules, and one draw needn't show every extreme that they name: `point_tile`: of the points of one device, at most 2 share one tile, and some tile receives exactly 2 of them.
All inputs are finite; a program needn't handle non-finite values. No bound on the sum of `wave_land` or of `ocean_land` on one device may be relied on, other than what follows from the above.
Results may differ from a plain program's by a relative error of at most 0.00071.
Values sent between devices are 32-bit elements; how exact they have to be, the bound alone decides.
A program may use at most 128 MiB of HBM per device.

v0:
```python
import jax
import jax.numpy as jnp
from jax import lax
from jax.experimental import pallas as pl
from jax.experimental.pallas import tpu as pltpu
from jax.sharding import PartitionSpec as P

ALL = ("mp", "gx", "gy")
F32 = jnp.float32
BF16 = jnp.bfloat16
MESH = pl.DeviceIdType.MESH

BINS = 1152
PTS = 128
LEV = 32
PLANES = 64
DEVS = 128
ROWS = 16
COLS = 8
PAD = 144
CHUNK = 72
MROWS = 384


def near(a):
    return min(a, 4 - a)


OFFSETS = sorted(
    [
        (dx, dy, dz, dc)
        for dx in range(4)
        for dy in range(4)
        for dz in range(4)
        for dc in range(2)
        if (dx, dy, dz, dc) != (0, 0, 0, 0)
    ],
    key=lambda d: (-(near(d[0]) + near(d[1]) + near(d[2])), d),
)


def split(x):
    high = x.astype(BF16)
    low = (x - high.astype(F32)).astype(BF16)
    return high, low


def dot_nt(a, b):
    return lax.dot_general(a, b, (((1,), (1,)), ((), ())), preferred_element_type=F32)


def dot_tn(a, b):
    return lax.dot_general(a, b, (((0,), (0,)), ((), ())), preferred_element_type=F32)


def dot_nn(a, b):
    return jnp.dot(a, b, preferred_element_type=F32)


def kernel(
    spec_h, w_h, dw_h, cour_v, tile_v, cell_v, land_v, vel_h, oland_h,
    eout_h, oout_h,
    e_v, c_v, g_v, lin_v, w_v, dw_v, cx_v, cy_v, oa_v, ob_v, f_v, sea_v, ol_v,
    q_v, rt_v, rs_v, cc_v, at_v,
    s1, r1, s2, r2, s3, r3, s4, r4,
    rowp, rowr, colp, colr, hc_v,
    wrp, wrr, wcp, wcr,
    in_sem, w_sem, out_sem, a_send, a_recv, h_send, h_recv, g_send, g_recv,
):
    mp, gx, gy = lax.axis_index("mp"), lax.axis_index("gx"), lax.axis_index("gy")
    row = mp * 8 + gx
    me = row * 8 + gy
    px, pz, py, pc = mp * 2 + gx % 2, gx // 2, gy // 2, gy % 2

    in_e = pltpu.make_async_copy(spec_h, e_v, in_sem.at[0])
    in_dw = pltpu.make_async_copy(dw_h, dw_v, in_sem.at[1])
    in_ol = pltpu.make_async_copy(oland_h, ol_v, in_sem.at[2])
    in_u = pltpu.make_async_copy(vel_h, oa_v.at[:, pl.ds(8, 128), :], in_sem.at[3])
    in_e.start()
    in_dw.start()
    in_u.start()
    in_ol.start()
    in_w = [pltpu.make_async_copy(w_h.at[m], w_v.at[m], w_sem.at[m]) for m in range(4)]
    for copy in in_w:
        copy.start()

    barrier = pltpu.get_barrier_semaphore()

    def greet(i, carry):
        p = (me + i) % DEVS
        pl.semaphore_signal(
            barrier, inc=1, device_id=(p // 64, (p // 8) % 8, p % 8), device_id_type=MESH
        )
        return carry

    lax.fori_loop(1, DEVS, greet, 0)

    lane = lax.broadcasted_iota(jnp.int32, (128, 128), 1)
    sub = lax.broadcasted_iota(jnp.int32, (128, 128), 0)

    def exchange_all(n, src, dst):
        for dx, dy, dz, dc in OFFSETS:
            tx, ty, tz, tc = (px + dx) % 4, (py + dy) % 4, (pz + dz) % 4, (pc + dc) % 2
            to = (tx // 2, tz * 2 + tx % 2, ty * 2 + tc)
            peer = (to[0] * 8 + to[1]) * 8 + to[2]
            pltpu.make_async_remote_copy(
                src_ref=src.at[peer], dst_ref=dst.at[me],
                send_sem=a_send.at[n], recv_sem=a_recv.at[n],
                device_id=to, device_id_type=MESH,
            ).start()
        dst[pl.ds(me, 1)] = src[pl.ds(me, 1)]

    def exchange_sent(n, src):
        block = src.at[pl.ds(0, DEVS - 1)]
        pltpu.make_async_copy(block, block, a_send.at[n]).wait()

    def exchange_come(n, dst):
        block = dst.at[pl.ds(0, DEVS - 1)]
        pltpu.make_async_copy(block, block, a_recv.at[n]).wait()

    up, down = (row + ROWS - 1) % ROWS, (row + 1) % ROWS
    left, right = (gy + COLS - 1) % COLS, (gy + 1) % COLS
    at_up, at_down = (up // 8, up % 8, gy), (down // 8, down % 8, gy)
    at_left, at_right = (mp, gx, left), (mp, gx, right)

    def halo_copies(rows_out, rows_in, cols_out, cols_in, ss, rs, n):
        def one(k, src, dst, to):
            return pltpu.make_async_remote_copy(
                src_ref=src, dst_ref=dst, send_sem=ss.at[n, k], recv_sem=rs.at[n, k],
                device_id=to, device_id_type=MESH,
            )

        return [
            one(0, rows_out.at[0], rows_in.at[1], at_up),
            one(1, rows_out.at[1], rows_in.at[0], at_down),
            one(2, cols_out, cols_in.at[1], at_left),
            one(3, cols_out, cols_in.at[0], at_right),
        ]

    ocean_halo = [
        halo_copies(rowp.at[n], rowr.at[n], colp.at[n], colr.at[n], h_send, h_recv, n)
        for n in range(4)
    ]
    wave_halo = [
        halo_copies(wrp.at[n], wrr.at[n], wcp.at[n], wcr.at[n], g_send, g_recv, n)
        for n in range(2)
    ]
    has_up = (row > 0).astype(F32)
    has_down = (row < ROWS - 1).astype(F32)
    has_left = (gy > 0).astype(F32)
    has_right = (gy < COLS - 1).astype(F32)

    tile_row = jnp.broadcast_to(tile_v[...], (128, 128))
    tile_col = tile_row.T
    before = jnp.where((tile_row == tile_col) & (sub < lane), 1.0, 0.0)
    rank = jnp.sum(before, axis=0, keepdims=True)
    for r in range(2):
        mine = (tile_row == sub) & (jnp.broadcast_to(rank, (128, 128)) == float(r))
        q_v[r] = jnp.where(mine, 1.0, 0.0).astype(BF16)

    def drift_out(dst):
        d = dot_nn(dw_v[...], c_v[...])
        extra = jnp.broadcast_to((cell_v[...] + 1).astype(F32), (64, 128))
        high, low = split(jnp.concatenate([d, extra], axis=0))
        for r in range(2):
            dst[:, r, :] = dot_nt(q_v[r], high) + dot_nt(q_v[r], low)

    in_e.wait()
    in_dw.wait()
    c_v[...] = e_v[...].astype(BF16)
    drift_out(s1)

    for b in range(BINS // 128):
        block = pl.ds(b * 128, 128)
        cx_v[block, :] = jnp.broadcast_to(cour_v[0:1, block], (128, 128)).T
        cy_v[block, :] = jnp.broadcast_to(cour_v[1:2, block], (128, 128)).T

    in_ol.wait()
    sea_v[...] = ol_v[...].astype(F32) * 0.2
    in_u.wait()

    def insert(cols, x, p):
        here = (lane // 2) == p
        return jnp.where(here, pltpu.roll(x, 2 * p + 1, 1), cols)

    def pack_plane(n, p, x, cols):
        rowp[n, 0, pl.ds(p, 1), :] = x[0:1]
        rowp[n, 1, pl.ds(p, 1), :] = x[127:128]
        return insert(cols, x, p)

    def pack_first(p, cols):
        return pack_plane(0, p, oa_v[p, 8:136, :], cols)

    colp[0] = lax.fori_loop(0, PLANES, pack_first, jnp.zeros((128, 128), F32))

    def linear(first, last):
        def one(i, carry):
            m, b = i // 3, i % 3
            rows = pl.ds(pl.multiple_of(b * MROWS, MROWS), MROWS)
            lin_v[m, rows, :] = dot_nn(w_v[m, rows, :], c_v[...])
            return carry

        lax.fori_loop(first, last, one, 0)

    in_w[0].wait()
    linear(0, 3)
    pl.semaphore_wait(barrier, DEVS - 1)

    exchange_all(0, s1, r1)
    for copy in ocean_halo[0]:
        copy.start()
    for copy in in_w[1:]:
        copy.wait()
    linear(3, 12)

    exchange_come(0, r1)

    def arrived(src):
        return jnp.concatenate([src[:, 0, :], src[:, 1, :]], axis=0)

    a = arrived(r1)
    at = a.T
    at_v[...] = at[0:PLANES] * 0.5
    cell_t = at[64:65, :].astype(jnp.int32) - 1
    wide = lax.broadcasted_iota(jnp.int32, (128, 256), 0)
    rt_v[...] = jnp.where(wide == jnp.broadcast_to(cell_t >> 7, (128, 256)), 1.0, 0.0).astype(BF16)
    cell_c = jnp.broadcast_to(a[:, 64:65], (256, 128)).astype(jnp.int32) - 1
    tall = lax.broadcasted_iota(jnp.int32, (256, 128), 1)
    rs_v[...] = jnp.where(tall == (cell_c >> 7), 1.0, 0.0).astype(BF16)
    cc_v[...] = jnp.where(tall == (cell_c & 127), 1.0, 0.0).astype(BF16)

    def currents_out(ocean, dst):
        found = []
        for f in range(2):
            high, low = split(ocean[f * LEV, 8:136, :])
            x = dot_nn(rs_v[...], high) + dot_nn(rs_v[...], low)
            found.append(jnp.sum(x * cc_v[...].astype(F32), axis=1, keepdims=True))
        both = jnp.where(tall == 0, found[0], jnp.where(tall == 1, found[1], 0.0))
        dst[:, 0, :] = both[0:128]
        dst[:, 1, :] = both[128:256]

    currents_out(oa_v, s2)
    exchange_all(1, s2, r2)

    def forcing():
        def one(p, carry):
            high, low = split(jnp.broadcast_to(at_v[pl.ds(p, 1), :], (16, 256)))
            high = jnp.broadcast_to(high[0:1], (128, 256))
            low = jnp.broadcast_to(low[0:1], (128, 256))
            f_v[p] = dot_nn(rt_v[...] * high, cc_v[...]) + dot_nn(rt_v[...] * low, cc_v[...])
            return carry

        lax.fori_loop(0, PLANES, one, 0)

    def substep(n, src, dst, pack):
        for copy in ocean_halo[n]:
            copy.wait()
        even = (lane % 2) == 0
        hc_v[...] = jnp.where(
            even, colr[n, 0] * has_left, pltpu.roll(colr[n, 1], 126, 1) * has_right
        )

        def around(p):
            src[p, 7:8, :] = rowr[n, 0, pl.ds(p, 1), :] * has_up
            src[p, 136:137, :] = rowr[n, 1, pl.ds(p, 1), :] * has_down
            x = src[p, 8:136, :]
            edge = pltpu.roll(hc_v[...], (128 - 2 * p) % 128, 1)
            west = jnp.where(lane == 0, edge, pltpu.roll(x, 1, 1))
            east = jnp.where(lane == 127, edge, pltpu.roll(x, 127, 1))
            return x, (src[p, 7:135, :] + src[p, 9:137, :]) + (west + east) + x

        def one(l, cols):
            u, su = around(l)
            v, sv = around(LEV + l)
            un = sea_v[...] * (su + 0.5 * v + f_v[LEV + l])
            vn = sea_v[...] * (sv - 0.5 * u - f_v[l])
            dst[l, 8:136, :] = un
            dst[LEV + l, 8:136, :] = vn
            if pack:
                cols = pack_plane(n + 1, l, un, cols)
                cols = pack_plane(n + 1, LEV + l, vn, cols)
            return cols

        cols = lax.fori_loop(0, LEV, one, jnp.zeros((128, 128), F32))
        if pack:
            colp[n + 1] = cols
            for copy in ocean_halo[n + 1]:
                copy.start()

    sea_row = land_v[...].astype(F32)
    lane_c = lax.broadcasted_iota(jnp.int32, (CHUNK, 128), 1)
    seg = lane_c // 32
    pos = lane_c % 32

    def grow(n, src):
        exchange_come(2 * n + 1 if n == 0 else 3, src)
        now = jnp.zeros((128, 128), F32)
        for r in range(2):
            high, low = split(src[:, r, :])
            now = now + dot_tn(high, q_v[r]) + dot_tn(low, q_v[r])
        cu, cv = now[0:1], now[1:2]

        def one(k, carry):
            first = jnp.zeros((CHUNK, 128), F32)
            last = jnp.zeros((CHUNK, 128), F32)
            cols = carry
            for q in range(4):
                rows = pl.ds(pl.multiple_of(288 * q + CHUNK * k, 8), CHUNK)
                g = sea_row * (
                    e_v[rows, :]
                    + 0.1 * lin_v[0, rows, :] * lin_v[1, rows, :]
                    + 0.1 * (cu * lin_v[2, rows, :] + cv * lin_v[3, rows, :])
                )
                g_v[rows, :] = g
                first = jnp.where(seg == q, pltpu.roll(g, 32 * q, 1) if q else g, first)
                last = jnp.where(seg == q, pltpu.roll(g, (32 * q + 32) % 128, 1) if q < 3 else g, last)
                group = 4 * q + k
                cols = jnp.where(pos // 2 == group, pltpu.roll(g, 2 * group + 1, 1), cols)
            part = pl.ds(pl.multiple_of(CHUNK * k, 8), CHUNK)
            wrp[n, 0, part, :] = first
            wrp[n, 1, part, :] = last
            return cols

        wcp[n] = lax.fori_loop(0, 4, one, jnp.zeros((CHUNK, 128), F32))
        for copy in wave_halo[n]:
            copy.start()

    def advect(n):
        for copy in wave_halo[n]:
            copy.wait()
        cols = jnp.where(
            lane_c % 2 == 0,
            pltpu.roll(wcr[n, 0], 96, 1) * has_left,
            pltpu.roll(wcr[n, 1], 30, 1) * has_right,
        )
        flow_x = jnp.where(seg == 0, has_up, 1.0)
        flow_y = jnp.where(pos == 0, has_left, 1.0)

        def one(k, carry):
            part = pl.ds(pl.multiple_of(CHUNK * k, 8), CHUNK)
            above = wrr[n, 0, part, :] * has_up
            below = wrr[n, 1, part, :] * has_down
            for q in range(4):
                rows = pl.ds(pl.multiple_of(288 * q + CHUNK * k, 8), CHUNK)
                group = 4 * q + k
                g = g_v[rows, :]
                cx, cy = cx_v[rows, :], cy_v[rows, :]
                edge = pltpu.roll(cols, (128 - 2 * group) % 128, 1)
                g_down = jnp.where(
                    seg == 3, pltpu.roll(below, (96 - 32 * q) % 128, 1), pltpu.roll(g, 96, 1)
                )
                g_up = jnp.where(
                    seg == 0, pltpu.roll(above, (128 - 32 * q) % 128, 1), pltpu.roll(g, 32, 1)
                )
                g_right = jnp.where(pos == 31, edge, pltpu.roll(g, 127, 1))
                g_left = jnp.where(pos == 0, edge, pltpu.roll(g, 1, 1))
                px_, nx_ = jnp.maximum(cx, 0.0), jnp.minimum(cx, 0.0)
                py_, ny_ = jnp.maximum(cy, 0.0), jnp.minimum(cy, 0.0)
                out_x = px_ * g + nx_ * g_down
                in_x = flow_x * (px_ * g_up + nx_ * g)
                out_y = py_ * g + ny_ * g_right
                in_y = flow_y * (py_ * g_left + ny_ * g)
                e_v[rows, :] = sea_row * (g - (out_x - in_x) - (out_y - in_y))
            return carry

        lax.fori_loop(0, 4, one, 0)

    forcing()
    substep(0, oa_v, ob_v, True)
    grow(0, r2)
    substep(1, ob_v, oa_v, True)
    currents_out(oa_v, s4)
    exchange_all(3, s4, r4)
    advect(0)
    c_v[...] = e_v[...].astype(BF16)
    drift_out(s3)
    exchange_all(2, s3, r3)
    linear(0, 12)
    grow(1, r4)
    exchange_come(2, r3)
    at_v[...] = arrived(r3).T[0:PLANES] * 0.5
    forcing()
    substep(2, oa_v, ob_v, True)
    advect(1)
    out_e = pltpu.make_async_copy(e_v, eout_h, out_sem.at[0])
    out_e.start()
    substep(3, ob_v, oa_v, False)
    out_u = pltpu.make_async_copy(oa_v.at[:, pl.ds(8, 128), :], oout_h, out_sem.at[1])
    out_u.start()
    for n, src in enumerate((s1, s2, s3, s4)):
        exchange_sent(n, src)
    out_e.wait()
    out_u.wait()


def step(spectrum, weights, drift, courant, tile, cell, land, vel, oland):
    small = pl.BlockSpec(memory_space=pltpu.VMEM)
    far = pl.BlockSpec(memory_space=pl.ANY)
    v = pltpu.VMEM
    d = pltpu.SemaphoreType.DMA
    block = v((DEVS, 2, 128), F32)
    e, o = pl.pallas_call(
        kernel,
        out_shape=(
            jax.ShapeDtypeStruct((BINS, PTS), F32),
            jax.ShapeDtypeStruct((PLANES, 128, 128), F32),
        ),
        in_specs=[far, far, far, small, small, small, small, far, far],
        out_specs=(far, far),
        scratch_shapes=[
            v((BINS, 128), F32), v((BINS, 128), BF16), v((BINS, 128), F32),
            v((4, BINS, 128), F32), v((4, BINS, BINS), BF16), v((PLANES, BINS), BF16),
            v((BINS, 128), F32), v((BINS, 128), F32),
            v((PLANES, PAD, 128), F32), v((PLANES, PAD, 128), F32),
            v((PLANES, 128, 128), F32), v((128, 128), F32), v((128, 128), jnp.int32),
            v((2, 128, 128), BF16), v((128, 256), BF16), v((256, 128), BF16),
            v((256, 128), BF16), v((PLANES, 256), F32),
            block, block, block, block, block, block, block, block,
            v((4, 2, PLANES, 128), F32), v((4, 2, PLANES, 128), F32),
            v((4, 128, 128), F32), v((4, 2, 128, 128), F32), v((128, 128), F32),
            v((2, 2, 288, 128), F32), v((2, 2, 288, 128), F32),
            v((2, CHUNK, 128), F32), v((2, 2, CHUNK, 128), F32),
            d((4,)), d((4,)), d((2,)), d((4,)), d((4,)),
            d((4, 4)), d((4, 4)), d((2, 4)), d((2, 4)),
        ],
        name="coupled",
        compiler_params=pltpu.CompilerParams(
            collective_id=0, has_side_effects=True, vmem_limit_bytes=60 * 1024 * 1024
        ),
    )(
        spectrum, weights, drift, courant,
        tile.reshape(1, PTS), cell.reshape(1, PTS), land.reshape(1, PTS),
        vel.reshape(PLANES, 128, 128), oland,
    )
    return e, o.reshape(2, LEV, 128, 128)


def solution(mesh):
    ocean = P(None, None, ("mp", "gx"), "gy")
    return jax.shard_map(
        step,
        mesh=mesh,
        in_specs=(
            P(None, ALL), P(), P(), P(), P(ALL, None), P(ALL), P(ALL),
            ocean, P(("mp", "gx"), "gy"),
        ),
        out_specs=(P(None, ALL), ocean),
        check_vma=False,
    )
```

profile of v0, /device:TPU:0, one launch (start us, length us, event | category | flops | bytes accessed | tf_op | source)
XLA Modules:
  0.0 107.0 jit_solution(12888899367786472857)
XLA Ops:
  0.6 99.7 %coupled.1 = (f32[1152,128]{1,0:T(8,128)}, f32[64,128,128]{2,1,0:T(8,128)}) custom-call(f32[1152,128]{1,0:T(8,128)} %spec_h.1, bf16[4,1152,1152]{2,1,0:T(8,128)(2,1)} %w_h.1, bf16[64,1152]{1,0:T(8,128)(2,1)} %dw_h.1, f32[2,1152]{1,0:T(2,128)} %cour_v.1, s32[1,128]{1,0:T(1,128)} %bitcast.7, s32[1,128]{1,0:T(1,128)} %bitcast.8, s32[1,128]{1,0:T(1,128)} %bitcast.9, ...), custom_call_target="tpu_custom_call" | custom-call | tf_op jit(solution)/shard_map/coupled/pallas_call | solution.py:402
  100.3 1.9 %copy.13 = f32[1152,128]{1,0:T(8,128)} copy(f32[1152,128]{1,0:T(8,128)} %get-tuple-element.8) | data formatting | bytes 1179648
  102.3 4.7 %copy.14 = f32[2,32,128,128]{3,2,1,0:T(8,128)} copy(f32[2,32,128,128]{3,2,1,0:T(8,128)} %bitcast.5) | data formatting | bytes 8388608
where the time goes:
time: 107 us
  Pallas kernels  99.7 us (93%)
  local copies, waits for them, and re-layouts  6.61 us (6%)
    pallas_call x1, Pallas kernels, step(): pl.pallas_call(kernel, out_shape=(jax.ShapeDtypeStruct((BINS, PTS), F32),...  99.7 us
    unnamed x2, local copies, waits for them, and re-layouts  6.61 us

commit v1 on v0

--- a/solution.py
+++ b/solution.py
@@ -20,6 +20,8 @@
 PAD = 144
 CHUNK = 72
 MROWS = 384
+STRIP = 128
+UNROLL = 4
 
 
 def near(a):
@@ -39,6 +41,10 @@
 )
 
 
+def place(x, y, z, core):
+    return (x // 2, z * 2 + x % 2, y * 2 + core)
+
+
 def split(x):
     high = x.astype(BF16)
     low = (x - high.astype(F32)).astype(BF16)
@@ -60,7 +66,7 @@
 def kernel(
     spec_h, w_h, dw_h, cour_v, tile_v, cell_v, land_v, vel_h, oland_h,
     eout_h, oout_h,
-    e_v, c_v, g_v, lin_v, w_v, dw_v, cx_v, cy_v, oa_v, ob_v, f_v, sea_v, ol_v,
+    e_v, c_v, g_v, lin_v, w_v, dw_v, cx_v, cy_v, oa_v, ob_v, f_v, sea_v, ol_v, tri_v,
     q_v, rt_v, rs_v, cc_v, at_v,
     s1, r1, s2, r2, s3, r3, s4, r4,
     rowp, rowr, colp, colr, hc_v,
@@ -86,22 +92,16 @@
 
     barrier = pltpu.get_barrier_semaphore()
 
-    def greet(i, carry):
-        p = (me + i) % DEVS
-        pl.semaphore_signal(
-            barrier, inc=1, device_id=(p // 64, (p // 8) % 8, p % 8), device_id_type=MESH
-        )
-        return carry
-
-    lax.fori_loop(1, DEVS, greet, 0)
+    for dx, dy, dz, dc in OFFSETS:
+        to = place((px + dx) % 4, (py + dy) % 4, (pz + dz) % 4, (pc + dc) % 2)
+        pl.semaphore_signal(barrier, inc=1, device_id=to, device_id_type=MESH)
 
     lane = lax.broadcasted_iota(jnp.int32, (128, 128), 1)
     sub = lax.broadcasted_iota(jnp.int32, (128, 128), 0)
 
     def exchange_all(n, src, dst):
         for dx, dy, dz, dc in OFFSETS:
-            tx, ty, tz, tc = (px + dx) % 4, (py + dy) % 4, (pz + dz) % 4, (pc + dc) % 2
-            to = (tx // 2, tz * 2 + tx % 2, ty * 2 + tc)
+            to = place((px + dx) % 4, (py + dy) % 4, (pz + dz) % 4, (pc + dc) % 2)
             peer = (to[0] * 8 + to[1]) * 8 + to[2]
             pltpu.make_async_remote_copy(
                 src_ref=src.at[peer], dst_ref=dst.at[me],
@@ -175,23 +175,32 @@
         cx_v[block, :] = jnp.broadcast_to(cour_v[0:1, block], (128, 128)).T
         cy_v[block, :] = jnp.broadcast_to(cour_v[1:2, block], (128, 128)).T
 
+    deep = lax.broadcasted_iota(jnp.int32, (256, 128), 0) & 127
+    tall = lax.broadcasted_iota(jnp.int32, (256, 128), 1)
+    tri_v[...] = jnp.where((deep - tall == 1) | (tall - deep == 1), 1.0, 0.0).astype(BF16)
     in_ol.wait()
     sea_v[...] = ol_v[...].astype(F32) * 0.2
-    in_u.wait()
-
-    def insert(cols, x, p):
-        here = (lane // 2) == p
-        return jnp.where(here, pltpu.roll(x, 2 * p + 1, 1), cols)
-
-    def pack_plane(n, p, x, cols):
-        rowp[n, 0, pl.ds(p, 1), :] = x[0:1]
-        rowp[n, 1, pl.ds(p, 1), :] = x[127:128]
-        return insert(cols, x, p)
-
-    def pack_first(p, cols):
-        return pack_plane(0, p, oa_v[p, 8:136, :], cols)
-
-    colp[0] = lax.fori_loop(0, PLANES, pack_first, jnp.zeros((128, 128), F32))
+
+    lane_s = lax.broadcasted_iota(jnp.int32, (STRIP, 128), 1)
+
+    def pack_plane(n, p, s, x):
+        if s == 0:
+            rowp[n, 0, pl.ds(p, 1), :] = x[0:1]
+        if s == 128 // STRIP - 1:
+            rowp[n, 1, pl.ds(p, 1), :] = x[STRIP - 1 : STRIP]
+        pltpu.store(
+            colp.at[n, pl.ds(s * STRIP, STRIP), :],
+            pltpu.roll(x, 2 * p + 1, 1),
+            mask=(lane_s >> 1) == p,
+        )
+
+    def pack_first(p, carry):
+        for s in range(128 // STRIP):
+            pack_plane(0, p, s, oa_v[p, 8 + s * STRIP : 8 + (s + 1) * STRIP, :])
+        return carry
+
+    def pack_start():
+        lax.fori_loop(0, PLANES, pack_first, 0, unroll=4)
 
     def linear(first, last):
         def one(i, carry):
@@ -205,8 +214,9 @@
     in_w[0].wait()
     linear(0, 3)
     pl.semaphore_wait(barrier, DEVS - 1)
-
     exchange_all(0, s1, r1)
+    in_u.wait()
+    pack_start()
     for copy in ocean_halo[0]:
         copy.start()
     for copy in in_w[1:]:
@@ -225,7 +235,6 @@
     wide = lax.broadcasted_iota(jnp.int32, (128, 256), 0)
     rt_v[...] = jnp.where(wide == jnp.broadcast_to(cell_t >> 7, (128, 256)), 1.0, 0.0).astype(BF16)
     cell_c = jnp.broadcast_to(a[:, 64:65], (256, 128)).astype(jnp.int32) - 1
-    tall = lax.broadcasted_iota(jnp.int32, (256, 128), 1)
     rs_v[...] = jnp.where(tall == (cell_c >> 7), 1.0, 0.0).astype(BF16)
     cc_v[...] = jnp.where(tall == (cell_c & 127), 1.0, 0.0).astype(BF16)
 
@@ -250,40 +259,43 @@
             f_v[p] = dot_nn(rt_v[...] * high, cc_v[...]) + dot_nn(rt_v[...] * low, cc_v[...])
             return carry
 
-        lax.fori_loop(0, PLANES, one, 0)
+        lax.fori_loop(0, PLANES, one, 0, unroll=16)
 
     def substep(n, src, dst, pack):
         for copy in ocean_halo[n]:
             copy.wait()
+        src[:, 7, :] = rowr[n, 0] * has_up
+        src[:, 136, :] = rowr[n, 1] * has_down
         even = (lane % 2) == 0
         hc_v[...] = jnp.where(
             even, colr[n, 0] * has_left, pltpu.roll(colr[n, 1], 126, 1) * has_right
         )
 
+        brim = (lane == 0) | (lane == 127)
+
         def around(p):
-            src[p, 7:8, :] = rowr[n, 0, pl.ds(p, 1), :] * has_up
-            src[p, 136:137, :] = rowr[n, 1, pl.ds(p, 1), :] * has_down
             x = src[p, 8:136, :]
-            edge = pltpu.roll(hc_v[...], (128 - 2 * p) % 128, 1)
-            west = jnp.where(lane == 0, edge, pltpu.roll(x, 1, 1))
-            east = jnp.where(lane == 127, edge, pltpu.roll(x, 127, 1))
-            return x, (src[p, 7:135, :] + src[p, 9:137, :]) + (west + east) + x
-
-        def one(l, cols):
+            high, low = split(x)
+            across = dot_nn(jnp.concatenate([high, low], axis=1), tri_v[...])
+            edge = jnp.where(brim, pltpu.roll(hc_v[...], (128 - 2 * p) % 128, 1), 0.0)
+            return x, (src[p, 7:135, :] + src[p, 9:137, :]) + (x + edge) + across
+
+        def one(l, carry):
             u, su = around(l)
             v, sv = around(LEV + l)
-            un = sea_v[...] * (su + 0.5 * v + f_v[LEV + l])
-            vn = sea_v[...] * (sv - 0.5 * u - f_v[l])
+            un = sea_v[...] * (su + (0.5 * v + f_v[LEV + l]))
+            vn = sea_v[...] * (sv - (0.5 * u + f_v[l]))
             dst[l, 8:136, :] = un
             dst[LEV + l, 8:136, :] = vn
             if pack:
-                cols = pack_plane(n + 1, l, un, cols)
-                cols = pack_plane(n + 1, LEV + l, vn, cols)
-            return cols
-
-        cols = lax.fori_loop(0, LEV, one, jnp.zeros((128, 128), F32))
+                for s in range(128 // STRIP):
+                    rows = slice(s * STRIP, (s + 1) * STRIP)
+                    pack_plane(n + 1, l, s, un[rows])
+                    pack_plane(n + 1, LEV + l, s, vn[rows])
+            return carry
+
+        lax.fori_loop(0, LEV, one, 0, unroll=UNROLL)
         if pack:
-            colp[n + 1] = cols
             for copy in ocean_halo[n + 1]:
                 copy.start()
 
@@ -369,24 +381,25 @@
     substep(0, oa_v, ob_v, True)
     grow(0, r2)
     substep(1, ob_v, oa_v, True)
-    currents_out(oa_v, s4)
-    exchange_all(3, s4, r4)
     advect(0)
     c_v[...] = e_v[...].astype(BF16)
     drift_out(s3)
     exchange_all(2, s3, r3)
-    linear(0, 12)
-    grow(1, r4)
+    currents_out(oa_v, s4)
+    exchange_all(3, s4, r4)
+    linear(0, 8)
     exchange_come(2, r3)
     at_v[...] = arrived(r3).T[0:PLANES] * 0.5
     forcing()
     substep(2, oa_v, ob_v, True)
+    linear(8, 12)
+    grow(1, r4)
+    substep(3, ob_v, oa_v, False)
+    out_u = pltpu.make_async_copy(oa_v.at[:, pl.ds(8, 128), :], oout_h, out_sem.at[1])
+    out_u.start()
     advect(1)
     out_e = pltpu.make_async_copy(e_v, eout_h, out_sem.at[0])
     out_e.start()
-    substep(3, ob_v, oa_v, False)
-    out_u = pltpu.make_async_copy(oa_v.at[:, pl.ds(8, 128), :], oout_h, out_sem.at[1])
-    out_u.start()
     for n, src in enumerate((s1, s2, s3, s4)):
         exchange_sent(n, src)
     out_e.wait()
@@ -412,7 +425,7 @@
             v((4, BINS, 128), F32), v((4, BINS, BINS), BF16), v((PLANES, BINS), BF16),
             v((BINS, 128), F32), v((BINS, 128), F32),
             v((PLANES, PAD, 128), F32), v((PLANES, PAD, 128), F32),
-            v((PLANES, 128, 128), F32), v((128, 128), F32), v((128, 128), jnp.int32),
+            v((PLANES, 128, 128), F32), v((128, 128), F32), v((128, 128), jnp.int32), v((256, 128), BF16),
             v((2, 128, 128), BF16), v((128, 256), BF16), v((256, 128), BF16),
             v((256, 128), BF16), v((PLANES, 256), F32),
             block, block, block, block, block, block, block, block,

time: 107 us -> 71.5 us (0.67)
  the two profiles are of different devices: /device:TPU:0 before, /device:TPU:32 now
where the time goes in v1:
time: 71.5 us; the launch traced here: 71.3 us
  Pallas kernels  64 us (90%)
  local copies, waits for them, and re-layouts  6.61 us (9%)
    pallas_call x1, Pallas kernels, step(): pl.pallas_call(kernel, out_shape=(jax.ShapeDtypeStruct((BINS, PTS), F32),...  64 us
    unnamed x2, local copies, waits for them, and re-layouts  6.61 us

profile of v1, /device:TPU:32, one launch (start us, length us, event | category | flops | bytes accessed | tf_op | source)
XLA Modules:
  0.0 71.3 jit_solution(14312016067072021700)
XLA Ops:
  0.6 64.0 %coupled.1 = (f32[1152,128]{1,0:T(8,128)}, f32[64,128,128]{2,1,0:T(8,128)}) custom-call(f32[1152,128]{1,0:T(8,128)} %spec_h.1, bf16[4,1152,1152]{2,1,0:T(8,128)(2,1)} %w_h.1, bf16[64,1152]{1,0:T(8,128)(2,1)} %dw_h.1, f32[2,1152]{1,0:T(2,128)} %cour_v.1, s32[1,128]{1,0:T(1,128)} %bitcast.7, s32[1,128]{1,0:T(1,128)} %bitcast.8, s32[1,128]{1,0:T(1,128)} %bitcast.9, ...), custom_call_target="tpu_custom_call" | custom-call | tf_op jit(solution)/shard_map/coupled/pallas_call | solution.py:415
  64.7 1.9 %copy.13 = f32[1152,128]{1,0:T(8,128)} copy(f32[1152,128]{1,0:T(8,128)} %get-tuple-element.8) | data formatting | bytes 1179648
  66.6 4.7 %copy.14 = f32[2,32,128,128]{3,2,1,0:T(8,128)} copy(f32[2,32,128,128]{3,2,1,0:T(8,128)} %bitcast.5) | data formatting | bytes 8388608

commit v2 on v1

--- a/solution.py
+++ b/solution.py
@@ -64,14 +64,14 @@
 
 
 def kernel(
-    spec_h, w_h, dw_h, cour_v, tile_v, cell_v, land_v, vel_h, oland_h,
-    eout_h, oout_h,
+    spec_h, w_h, dw_h, cour_h, tile_h, cell_h, land_h, vel_h, oland_h,
+    eout_v, oout_v,
     e_v, c_v, g_v, lin_v, w_v, dw_v, cx_v, cy_v, oa_v, ob_v, f_v, sea_v, ol_v, tri_v,
-    q_v, rt_v, rs_v, cc_v, at_v,
+    q_v, rt_v, rs_v, cc_v, at_v, cour_v, tile_v, cell_v, land_v,
     s1, r1, s2, r2, s3, r3, s4, r4,
     rowp, rowr, colp, colr, hc_v,
     wrp, wrr, wcp, wcr,
-    in_sem, w_sem, out_sem, a_send, a_recv, h_send, h_recv, g_send, g_recv,
+    in_sem, w_sem, a_send, a_recv, h_send, h_recv, g_send, g_recv,
 ):
     mp, gx, gy = lax.axis_index("mp"), lax.axis_index("gx"), lax.axis_index("gy")
     row = mp * 8 + gx
@@ -82,6 +82,14 @@
     in_dw = pltpu.make_async_copy(dw_h, dw_v, in_sem.at[1])
     in_ol = pltpu.make_async_copy(oland_h, ol_v, in_sem.at[2])
     in_u = pltpu.make_async_copy(vel_h, oa_v.at[:, pl.ds(8, 128), :], in_sem.at[3])
+    in_small = [
+        pltpu.make_async_copy(src, dst, in_sem.at[4 + k])
+        for k, (src, dst) in enumerate(
+            ((tile_h, tile_v), (cell_h, cell_v), (land_h, land_v), (cour_h, cour_v))
+        )
+    ]
+    for copy in in_small:
+        copy.start()
     in_e.start()
     in_dw.start()
     in_u.start()
@@ -150,6 +158,8 @@
     has_left = (gy > 0).astype(F32)
     has_right = (gy < COLS - 1).astype(F32)
 
+    for copy in in_small:
+        copy.wait()
     tile_row = jnp.broadcast_to(tile_v[...], (128, 128))
     tile_col = tile_row.T
     before = jnp.where((tile_row == tile_col) & (sub < lane), 1.0, 0.0)
@@ -169,17 +179,6 @@
     in_dw.wait()
     c_v[...] = e_v[...].astype(BF16)
     drift_out(s1)
-
-    for b in range(BINS // 128):
-        block = pl.ds(b * 128, 128)
-        cx_v[block, :] = jnp.broadcast_to(cour_v[0:1, block], (128, 128)).T
-        cy_v[block, :] = jnp.broadcast_to(cour_v[1:2, block], (128, 128)).T
-
-    deep = lax.broadcasted_iota(jnp.int32, (256, 128), 0) & 127
-    tall = lax.broadcasted_iota(jnp.int32, (256, 128), 1)
-    tri_v[...] = jnp.where((deep - tall == 1) | (tall - deep == 1), 1.0, 0.0).astype(BF16)
-    in_ol.wait()
-    sea_v[...] = ol_v[...].astype(F32) * 0.2
 
     lane_s = lax.broadcasted_iota(jnp.int32, (STRIP, 128), 1)
 
@@ -219,6 +218,17 @@
     pack_start()
     for copy in ocean_halo[0]:
         copy.start()
+    for b in range(BINS // 128):
+        block = pl.ds(b * 128, 128)
+        cx_v[block, :] = jnp.broadcast_to(cour_v[0:1, block], (128, 128)).T
+        cy_v[block, :] = jnp.broadcast_to(cour_v[1:2, block], (128, 128)).T
+
+    deep = lax.broadcasted_iota(jnp.int32, (256, 128), 0) & 127
+    tall = lax.broadcasted_iota(jnp.int32, (256, 128), 1)
+    tri_v[...] = jnp.where((deep - tall == 1) | (tall - deep == 1), 1.0, 0.0).astype(BF16)
+    in_ol.wait()
+    sea_v[...] = ol_v[...].astype(F32) * 0.2
+
     for copy in in_w[1:]:
         copy.wait()
     linear(3, 12)
@@ -285,8 +295,12 @@
             v, sv = around(LEV + l)
             un = sea_v[...] * (su + (0.5 * v + f_v[LEV + l]))
             vn = sea_v[...] * (sv - (0.5 * u + f_v[l]))
-            dst[l, 8:136, :] = un
-            dst[LEV + l, 8:136, :] = vn
+            if pack:
+                dst[l, 8:136, :] = un
+                dst[LEV + l, 8:136, :] = vn
+            else:
+                dst[l] = un
+                dst[LEV + l] = vn
             if pack:
                 for s in range(128 // STRIP):
                     rows = slice(s * STRIP, (s + 1) * STRIP)
@@ -337,7 +351,7 @@
         for copy in wave_halo[n]:
             copy.start()
 
-    def advect(n):
+    def advect(n, dst):
         for copy in wave_halo[n]:
             copy.wait()
         cols = jnp.where(
@@ -372,7 +386,7 @@
                 in_x = flow_x * (px_ * g_up + nx_ * g)
                 out_y = py_ * g + ny_ * g_right
                 in_y = flow_y * (py_ * g_left + ny_ * g)
-                e_v[rows, :] = sea_row * (g - (out_x - in_x) - (out_y - in_y))
+                dst[rows, :] = sea_row * (g - (out_x - in_x) - (out_y - in_y))
             return carry
 
         lax.fori_loop(0, 4, one, 0)
@@ -381,45 +395,46 @@
     substep(0, oa_v, ob_v, True)
     grow(0, r2)
     substep(1, ob_v, oa_v, True)
-    advect(0)
+    currents_out(oa_v, s4)
+    exchange_all(3, s4, r4)
+    advect(0, e_v)
     c_v[...] = e_v[...].astype(BF16)
     drift_out(s3)
     exchange_all(2, s3, r3)
-    currents_out(oa_v, s4)
-    exchange_all(3, s4, r4)
-    linear(0, 8)
+    linear(0, 12)
+    grow(1, r4)
     exchange_come(2, r3)
     at_v[...] = arrived(r3).T[0:PLANES] * 0.5
     forcing()
     substep(2, oa_v, ob_v, True)
-    linear(8, 12)
-    grow(1, r4)
-    substep(3, ob_v, oa_v, False)
-    out_u = pltpu.make_async_copy(oa_v.at[:, pl.ds(8, 128), :], oout_h, out_sem.at[1])
-    out_u.start()
-    advect(1)
-    out_e = pltpu.make_async_copy(e_v, eout_h, out_sem.at[0])
-    out_e.start()
+    advect(1, eout_v)
+    substep(3, ob_v, oout_v, False)
     for n, src in enumerate((s1, s2, s3, s4)):
         exchange_sent(n, src)
-    out_e.wait()
-    out_u.wait()
 
 
 def step(spectrum, weights, drift, courant, tile, cell, land, vel, oland):
-    small = pl.BlockSpec(memory_space=pltpu.VMEM)
-    far = pl.BlockSpec(memory_space=pl.ANY)
+    near_by = pl.BlockSpec(memory_space=pltpu.VMEM)
+    far = pl.BlockSpec(memory_space=pltpu.HBM)
     v = pltpu.VMEM
     d = pltpu.SemaphoreType.DMA
     block = v((DEVS, 2, 128), F32)
+    args = [
+        pltpu.with_memory_space_constraint(x, pltpu.HBM)
+        for x in (
+            spectrum, weights, drift, courant,
+            tile.reshape(1, PTS), cell.reshape(1, PTS), land.reshape(1, PTS),
+            vel.reshape(PLANES, 128, 128), oland,
+        )
+    ]
     e, o = pl.pallas_call(
         kernel,
         out_shape=(
             jax.ShapeDtypeStruct((BINS, PTS), F32),
             jax.ShapeDtypeStruct((PLANES, 128, 128), F32),
         ),
-        in_specs=[far, far, far, small, small, small, small, far, far],
-        out_specs=(far, far),
+        in_specs=[far] * 9,
+        out_specs=(near_by, near_by),
         scratch_shapes=[
             v((BINS, 128), F32), v((BINS, 128), BF16), v((BINS, 128), F32),
             v((4, BINS, 128), F32), v((4, BINS, BINS), BF16), v((PLANES, BINS), BF16),
@@ -428,23 +443,20 @@
             v((PLANES, 128, 128), F32), v((128, 128), F32), v((128, 128), jnp.int32), v((256, 128), BF16),
             v((2, 128, 128), BF16), v((128, 256), BF16), v((256, 128), BF16),
             v((256, 128), BF16), v((PLANES, 256), F32),
+            v((2, BINS), F32), v((1, PTS), jnp.int32), v((1, PTS), jnp.int32), v((1, PTS), jnp.int32),
             block, block, block, block, block, block, block, block,
             v((4, 2, PLANES, 128), F32), v((4, 2, PLANES, 128), F32),
             v((4, 128, 128), F32), v((4, 2, 128, 128), F32), v((128, 128), F32),
             v((2, 2, 288, 128), F32), v((2, 2, 288, 128), F32),
             v((2, CHUNK, 128), F32), v((2, 2, CHUNK, 128), F32),
-            d((4,)), d((4,)), d((2,)), d((4,)), d((4,)),
+            d((8,)), d((4,)), d((4,)), d((4,)),
             d((4, 4)), d((4, 4)), d((2, 4)), d((2, 4)),
         ],
         name="coupled",
         compiler_params=pltpu.CompilerParams(
-            collective_id=0, has_side_effects=True, vmem_limit_bytes=60 * 1024 * 1024
+            collective_id=0, has_side_effects=True, vmem_limit_bytes=42 * 1024 * 1024
         ),
-    )(
-        spectrum, weights, drift, courant,
-        tile.reshape(1, PTS), cell.reshape(1, PTS), land.reshape(1, PTS),
-        vel.reshape(PLANES, 128, 128), oland,
-    )
+    )(*args)
     return e, o.reshape(2, LEV, 128, 128)
 
 

time: 71.5 us -> 61.4 us (0.86)
  the two profiles are of different devices: /device:TPU:32 before, /device:TPU:0 now
where the time goes in v2:
time: 61.4 us; the launch traced here: 61.3 us
  Pallas kernels  57.8 us (94%)
  local copies, waits for them, and re-layouts  2.83 us (5%)
  between operations  0.64 us (1%)
    pallas_call x1, Pallas kernels, step(): pl.pallas_call(kernel, out_shape=(jax.ShapeDtypeStruct((BINS, PTS), F32),...  57.8 us
    unnamed x2, local copies, waits for them, and re-layouts  2.83 us

profile of v2, /device:TPU:0, one launch (start us, length us, event | category | flops | bytes accessed | tf_op | source)
XLA Modules:
  0.0 61.3 jit_solution(1772046073256147049)
XLA Ops:
  0.6 57.8 %coupled.1 = (f32[1152,128]{1,0:T(8,128)S(1)}, f32[64,128,128]{2,1,0:T(8,128)S(1)}) custom-call(f32[1152,128]{1,0:T(8,128)} %spec_h.1, bf16[4,1152,1152]{2,1,0:T(8,128)(2,1)} %w_h.1, bf16[64,1152]{1,0:T(8,128)(2,1)} %dw_h.1, f32[2,1152]{1,0:T(2,128)} %cour_h.1, s32[1,128]{1,0:T(1,128)} %bitcast.7, s32[1,128]{1,0:T(1,128)} %bitcast.8, s32[1,128]{1,0:T(1,128)} %bitcast.9, ...), custom_call_target="tpu_custom_call" | custom-call | tf_op jit(solution)/shard_map/coupled/pallas_call | solution.py:430
  58.4 0.8 %copy.13 = f32[1152,128]{1,0:T(8,128)} copy(f32[1152,128]{1,0:T(8,128)S(1)} %get-tuple-element.8) | data formatting | bytes 1179648
  59.3 2.0 %copy.14 = f32[2,32,128,128]{3,2,1,0:T(8,128)} copy(f32[2,32,128,128]{3,2,1,0:T(8,128)S(1)} %bitcast.5) | data formatting | bytes 8388608

commit v3 on v2

--- a/solution.py
+++ b/solution.py
@@ -22,6 +22,7 @@
 MROWS = 384
 STRIP = 128
 UNROLL = 4
+FUSED = (0, 2)
 
 
 def near(a):
@@ -261,12 +262,15 @@
     currents_out(oa_v, s2)
     exchange_all(1, s2, r2)
 
+    def force(p):
+        high, low = split(jnp.broadcast_to(at_v[pl.ds(p, 1), :], (16, 256)))
+        high = jnp.broadcast_to(high[0:1], (128, 256))
+        low = jnp.broadcast_to(low[0:1], (128, 256))
+        return dot_nn(rt_v[...] * high, cc_v[...]) + dot_nn(rt_v[...] * low, cc_v[...])
+
     def forcing():
         def one(p, carry):
-            high, low = split(jnp.broadcast_to(at_v[pl.ds(p, 1), :], (16, 256)))
-            high = jnp.broadcast_to(high[0:1], (128, 256))
-            low = jnp.broadcast_to(low[0:1], (128, 256))
-            f_v[p] = dot_nn(rt_v[...] * high, cc_v[...]) + dot_nn(rt_v[...] * low, cc_v[...])
+            f_v[p] = force(p)
             return carry
 
         lax.fori_loop(0, PLANES, one, 0, unroll=16)
@@ -293,8 +297,14 @@
         def one(l, carry):
             u, su = around(l)
             v, sv = around(LEV + l)
-            un = sea_v[...] * (su + (0.5 * v + f_v[LEV + l]))
-            vn = sea_v[...] * (sv - (0.5 * u + f_v[l]))
+            if n in FUSED:
+                fe, fn = force(l), force(LEV + l)
+                f_v[l] = fe
+                f_v[LEV + l] = fn
+            else:
+                fe, fn = f_v[l], f_v[LEV + l]
+            un = sea_v[...] * (su + (0.5 * v + fn))
+            vn = sea_v[...] * (sv - (0.5 * u + fe))
             if pack:
                 dst[l, 8:136, :] = un
                 dst[LEV + l, 8:136, :] = vn
@@ -391,7 +401,6 @@
 
         lax.fori_loop(0, 4, one, 0)
 
-    forcing()
     substep(0, oa_v, ob_v, True)
     grow(0, r2)
     substep(1, ob_v, oa_v, True)
@@ -405,7 +414,6 @@
     grow(1, r4)
     exchange_come(2, r3)
     at_v[...] = arrived(r3).T[0:PLANES] * 0.5
-    forcing()
     substep(2, oa_v, ob_v, True)
     advect(1, eout_v)
     substep(3, ob_v, oout_v, False)

time: 61.4 us -> 59 us (0.961)
  Pallas kernels: 57.8 us -> 55.4 us
    pallas_call x1, Pallas kernels: 57.8 us -> 55.4 us  [step(): pl.pallas_call(kernel, out_shape=(jax.ShapeDtypeStruct((BINS, PTS), F32),...]
where the time goes in v3:
time: 59 us; the launch traced here: 58.9 us
  Pallas kernels  55.4 us (94%)
  local copies, waits for them, and re-layouts  2.83 us (5%)
  between operations  0.64 us (1%)
    pallas_call x1, Pallas kernels, step(): pl.pallas_call(kernel, out_shape=(jax.ShapeDtypeStruct((BINS, PTS), F32),...  55.4 us
    unnamed x2, local copies, waits for them, and re-layouts  2.83 us

profile of v3, /device:TPU:0, one launch (start us, length us, event | category | flops | bytes accessed | tf_op | source)
XLA Modules:
  0.0 58.9 jit_solution(5789006292987377106)
XLA Ops:
  0.6 55.4 %coupled.1 = (f32[1152,128]{1,0:T(8,128)S(1)}, f32[64,128,128]{2,1,0:T(8,128)S(1)}) custom-call(f32[1152,128]{1,0:T(8,128)} %spec_h.1, bf16[4,1152,1152]{2,1,0:T(8,128)(2,1)} %w_h.1, bf16[64,1152]{1,0:T(8,128)(2,1)} %dw_h.1, f32[2,1152]{1,0:T(2,128)} %cour_h.1, s32[1,128]{1,0:T(1,128)} %bitcast.7, s32[1,128]{1,0:T(1,128)} %bitcast.8, s32[1,128]{1,0:T(1,128)} %bitcast.9, ...), custom_call_target="tpu_custom_call" | custom-call | tf_op jit(solution)/shard_map/coupled/pallas_call | solution.py:438
  56.1 0.8 %copy.13 = f32[1152,128]{1,0:T(8,128)} copy(f32[1152,128]{1,0:T(8,128)S(1)} %get-tuple-element.8) | data formatting | bytes 1179648
  56.9 2.0 %copy.14 = f32[2,32,128,128]{3,2,1,0:T(8,128)} copy(f32[2,32,128,128]{3,2,1,0:T(8,128)S(1)} %bitcast.5) | data formatting | bytes 8388608

commit v4 on v3

--- a/solution.py
+++ b/solution.py
@@ -211,8 +211,6 @@
 
         lax.fori_loop(first, last, one, 0)
 
-    in_w[0].wait()
-    linear(0, 3)
     pl.semaphore_wait(barrier, DEVS - 1)
     exchange_all(0, s1, r1)
     in_u.wait()
@@ -230,9 +228,9 @@
     in_ol.wait()
     sea_v[...] = ol_v[...].astype(F32) * 0.2
 
-    for copy in in_w[1:]:
+    for copy in in_w:
         copy.wait()
-    linear(3, 12)
+    linear(0, 9)
 
     exchange_come(0, r1)
 
@@ -261,6 +259,7 @@
 
     currents_out(oa_v, s2)
     exchange_all(1, s2, r2)
+    linear(9, 12)
 
     def force(p):
         high, low = split(jnp.broadcast_to(at_v[pl.ds(p, 1), :], (16, 256)))

time: 59 us -> 60.2 us (1.020)
  Pallas kernels: 55.4 us -> 56.6 us
    pallas_call x1, Pallas kernels: 55.4 us -> 56.6 us  [step(): pl.pallas_call(kernel, out_shape=(jax.ShapeDtypeStruct((BINS, PTS), F32),...]
where the time goes in v4:
time: 60.2 us; the launch traced here: 60.1 us
  Pallas kernels  56.6 us (94%)
  local copies, waits for them, and re-layouts  2.83 us (5%)
  between operations  0.64 us (1%)
    pallas_call x1, Pallas kernels, step(): pl.pallas_call(kernel, out_shape=(jax.ShapeDtypeStruct((BINS, PTS), F32),...  56.6 us
    unnamed x2, local copies, waits for them, and re-layouts  2.83 us

profile of v4, /device:TPU:0, one launch (start us, length us, event | category | flops | bytes accessed | tf_op | source)
XLA Modules:
  0.0 60.1 jit_solution(1809305706979117194)
XLA Ops:
  0.6 56.6 %coupled.1 = (f32[1152,128]{1,0:T(8,128)S(1)}, f32[64,128,128]{2,1,0:T(8,128)S(1)}) custom-call(f32[1152,128]{1,0:T(8,128)} %spec_h.1, bf16[4,1152,1152]{2,1,0:T(8,128)(2,1)} %w_h.1, bf16[64,1152]{1,0:T(8,128)(2,1)} %dw_h.1, f32[2,1152]{1,0:T(2,128)} %cour_h.1, s32[1,128]{1,0:T(1,128)} %bitcast.7, s32[1,128]{1,0:T(1,128)} %bitcast.8, s32[1,128]{1,0:T(1,128)} %bitcast.9, ...), custom_call_target="tpu_custom_call" | custom-call | tf_op jit(solution)/shard_map/coupled/pallas_call | solution.py:437
  57.3 0.8 %copy.13 = f32[1152,128]{1,0:T(8,128)} copy(f32[1152,128]{1,0:T(8,128)S(1)} %get-tuple-element.8) | data formatting | bytes 1179648
  58.1 2.0 %copy.14 = f32[2,32,128,128]{3,2,1,0:T(8,128)} copy(f32[2,32,128,128]{3,2,1,0:T(8,128)S(1)} %bitcast.5) | data formatting | bytes 8388608
